TPU v7x, 32 devices: a whole 2x2x4 slice. The times are simulated.
32 devices in a mesh: base: 16 (over z, x, core), chan: 2 (over y).
Axes of the slice: x: 2, y: 2, z: 4, core: 2. Of those that a mesh axis runs over, the one named last changes fastest.
Arguments:
- image0: float32 [2048, 2048], P(('base', 'chan')), may hold values from -6 to 6
- interp: float32 [16, 2, 256, 8, 256], P('base', 'chan'), may hold values from -0.375 to 0.375
- vis_weight: float32 [16, 2, 256, 8], P('base', 'chan'), may hold values from 0.2 to 5
- counts: int32 [16, 2, 256], P('base', 'chan'), may hold values from 1 to 8
- tile_index: int32 [16, 2, 256], P('base', 'chan'), may hold values from 0 to 511
Outputs:
- image_out: float32 [2048, 2048], P(('base', 'chan'))
- estimates: float32 [3], replicated
Inputs may be any that keep to these rules, and one draw needn't show every extreme that they name: `tile_index`: slot s of a device belongs to the spectrum block of device s // 8 of base+chan, base index major; the entry numbers the tile within that block. `counts`: visibility v of a slot is live when v < count.
All inputs are finite; a program needn't handle non-finite values.
Results may differ from a plain program's by a relative error of at most 0.00023.
Values sent between devices are 32-bit elements; how exact they have to be, the bound alone decides.
A program may use at most 128 MiB of HBM per device.

v0:
```python
import math
import jax
import jax.numpy as jnp
from jax import lax
from jax.sharding import PartitionSpec as P

TILE_V = 8
TILE_U = 32
ITERS = 3
PRECISION_LEVEL = lax.Precision.HIGHEST


def split_length(length):
    outer_len = 2 ** ((length.bit_length() - 1) // 2)
    return (outer_len, length // outer_len)


def angle_table(count_a, count_b, modulus, sign):
    left = jnp.arange(count_a, dtype=jnp.int32)[:, None]
    right = jnp.arange(count_b, dtype=jnp.int32)[None, :]
    angle = sign * 2.0 * math.pi / modulus * (left * right % modulus).astype(jnp.float32)
    return (jnp.cos(angle), jnp.sin(angle))


def transform_rows(real_part, imag_part, sign):
    row_count, length = real_part.shape
    outer_len, inner_len = split_length(length)
    cos_q, sin_q = angle_table(inner_len, inner_len, inner_len, sign)
    cos_t, sin_t = angle_table(inner_len, outer_len, length, sign)
    cos_p, sin_p = angle_table(outer_len, outer_len, outer_len, sign)
    real_in = real_part.reshape(row_count, inner_len, outer_len)
    first_re = jnp.einsum("kq,rqp->rkp", cos_q, real_in, precision=PRECISION_LEVEL)
    first_im = jnp.einsum("kq,rqp->rkp", sin_q, real_in, precision=PRECISION_LEVEL)
    if imag_part is not None:
        imag_in = imag_part.reshape(row_count, inner_len, outer_len)
        first_re = first_re - jnp.einsum("kq,rqp->rkp", sin_q, imag_in, precision=PRECISION_LEVEL)
        first_im = first_im + jnp.einsum("kq,rqp->rkp", cos_q, imag_in, precision=PRECISION_LEVEL)
    turned_re = first_re * cos_t - first_im * sin_t
    turned_im = first_re * sin_t + first_im * cos_t
    last_re = jnp.einsum("jp,rkp->rjk", cos_p, turned_re, precision=PRECISION_LEVEL) - jnp.einsum(
        "jp,rkp->rjk", sin_p, turned_im, precision=PRECISION_LEVEL
    )
    last_im = jnp.einsum("jp,rkp->rjk", cos_p, turned_im, precision=PRECISION_LEVEL) + jnp.einsum(
        "jp,rkp->rjk", sin_p, turned_re, precision=PRECISION_LEVEL
    )
    factor = 1.0 / math.sqrt(length)
    return (
        last_re.reshape(row_count, length) * factor,
        last_im.reshape(row_count, length) * factor,
    )


def transpose_global(real_part, imag_part):
    row_count, length = real_part.shape
    n_base = lax.axis_size("base")
    n_chan = lax.axis_size("chan")
    width = length // (n_base * n_chan)
    moved = (
        lax.all_to_all(
            lax.all_to_all(
                real_part.reshape(1, row_count, n_base, n_chan, width),
                "base",
                split_axis=2,
                concat_axis=0,
                tiled=True,
            ),
            "chan",
            split_axis=3,
            concat_axis=1,
            tiled=True,
        ),
        lax.all_to_all(
            lax.all_to_all(
                imag_part.reshape(1, row_count, n_base, n_chan, width),
                "base",
                split_axis=2,
                concat_axis=0,
                tiled=True,
            ),
            "chan",
            split_axis=3,
            concat_axis=1,
            tiled=True,
        ),
    )
    return (moved[0].reshape(length, width).T, moved[1].reshape(length, width).T)


def to_tiles(plane):
    row_count, length = plane.shape
    shaped = plane.reshape(row_count // TILE_V, TILE_V, length // TILE_U, TILE_U)
    return shaped.transpose(0, 2, 1, 3).reshape(-1, TILE_V * TILE_U)


def from_tiles(tiles, row_count, length):
    shaped = tiles.reshape(row_count // TILE_V, length // TILE_U, TILE_V, TILE_U)
    return shaped.transpose(0, 2, 1, 3).reshape(row_count, length)


def slot_work(sample_weights, masked_weight, sample_values):
    visible_samples = (
        jnp.einsum("gnz,gez->gen", sample_weights, sample_values, precision=PRECISION_LEVEL)
        * masked_weight[:, None, :]
    )
    return jnp.einsum("hbi,hyb->hyi", sample_weights, visible_samples, precision=PRECISION_LEVEL)


def total_squares(image):
    return lax.psum(jnp.sum(image * image), ("base", "chan"))


def per_device(image0, interp, vis_weight, counts, tile_index):
    n_base = lax.axis_size("base")
    n_chan = lax.axis_size("chan")
    row_count, length = image0.shape
    touch = tile_index.shape[2]
    slots_each = touch // (n_base * n_chan)
    vcap = interp.shape[3]
    cells = interp.shape[4]
    tiles_own = row_count // TILE_V * (length // TILE_U)
    live = (jnp.arange(vcap, dtype=jnp.int32)[None, :] < counts.reshape(touch, 1)).astype(
        jnp.float32
    )
    masked_weight = vis_weight.reshape(touch, vcap) * live
    sample_weights = interp.reshape(touch, vcap, cells)
    wanted = lax.all_to_all(
        lax.all_to_all(
            tile_index.reshape(n_base, n_chan, slots_each),
            "base",
            split_axis=0,
            concat_axis=0,
            tiled=True,
        ),
        "chan",
        split_axis=1,
        concat_axis=1,
        tiled=True,
    ).reshape(touch)
    onehot = (jnp.arange(tiles_own, dtype=jnp.int32)[:, None] == wanted[None, :]).astype(
        jnp.float32
    )
    moved = (
        lax.all_to_all(
            lax.all_to_all(
                sample_weights.reshape(n_base, n_chan, slots_each, vcap, cells),
                "base",
                split_axis=0,
                concat_axis=0,
                tiled=True,
            ),
            "chan",
            split_axis=1,
            concat_axis=1,
            tiled=True,
        ),
        lax.all_to_all(
            lax.all_to_all(
                masked_weight.reshape(n_base, n_chan, slots_each, vcap),
                "base",
                split_axis=0,
                concat_axis=0,
                tiled=True,
            ),
            "chan",
            split_axis=1,
            concat_axis=1,
            tiled=True,
        ),
    )
    sample_weights = moved[0].reshape(touch, vcap, cells)
    masked_weight = moved[1].reshape(touch, vcap)
    found = []
    current = image0 / jnp.sqrt(total_squares(image0))
    for iteration in range(ITERS):
        real_part, imag_part = transform_rows(current, None, -1.0)
        real_part, imag_part = transpose_global(real_part, imag_part)
        real_part, imag_part = transform_rows(real_part, imag_part, -1.0)
        tiles = jnp.stack([to_tiles(real_part), to_tiles(imag_part)], axis=1)
        sample_values = jnp.take(tiles, wanted, axis=0)
        gridded_plane = slot_work(sample_weights, masked_weight, sample_values)
        summed = jnp.einsum("ts,skc->tkc", onehot, gridded_plane, precision=PRECISION_LEVEL)
        real_part = from_tiles(summed[:, 0, :], row_count, length)
        imag_part = from_tiles(summed[:, 1, :], row_count, length)
        real_part, imag_part = transform_rows(real_part, imag_part, 1.0)
        real_part, imag_part = transpose_global(real_part, imag_part)
        real_part, imag_part = transform_rows(real_part, imag_part, 1.0)
        norm_value = jnp.sqrt(total_squares(real_part))
        found.append(norm_value)
        current = real_part / norm_value
    return (float(length) * current, jnp.stack(found))


def solution(mesh):
    placed = (
        P(("base", "chan"), None),
        P("base", "chan", None, None, None),
        P("base", "chan", None, None),
        P("base", "chan", None),
        P("base", "chan", None),
    )
    return jax.shard_map(
        per_device,
        mesh=mesh,
        in_specs=placed,
        out_specs=(P(("base", "chan"), None), P()),
        check_vma=False,
    )
```

profile of v0, /device:TPU:0, one launch (start us, length us, event | category | flops | bytes accessed | tf_op | source)
XLA Modules:
  0.0 998.7 jit_solution(13095551597312861529)
XLA Ops:
  3.3 7.4 all-to-all-start
  14.0 40.9 %psum.28 = f32[]{:T(128)} all-reduce(f32[]{:T(128)} %multiply_reduce_fusion.3), channel_id=1, replica_groups=mesh['base'=16,'chan'=2] {'base','chan'}, use_global_device_ids=true, to_apply=%region_1.0 | all-reduce | flops 1 | bytes 8 | tf_op jit(solution)/shard_map/psum | solution.py:109
  69.5 4.9 all-to-all-start.8
  81.7 6.5 all-to-all-start.2
  95.1 7.3 all-to-all-done.2
  111.5 9.4 all-to-all-done.4
  133.8 7.1 all-to-all-done.3
  140.9 10.1 %all_to_all.426 = f32[2,1,65536]{2,1,0:T(1,128)S(1)} all-to-all(f32[2,1,65536]{2,1,0:T(1,128)S(1)} %reshape.488), channel_id=1, replica_groups=mesh['base'=16,'chan'=2] {'chan'}, dimensions={0} | all-to-all | bytes 1048576 | tf_op jit(solution)/shard_map/all_to_all | solution.py:72
  151.1 4.9 all-to-all-start.6
  174.9 21.9 %all-to-all-done.6 = f32[16,2,8,8,256]{4,3,2,1,0:T(8,128)} async-done(((f32[16,2,8,8,256]{4,3,2,1,0:T(8,128)}), f32[16,2,8,8,256]{4,3,2,1,0:T(8,128)}, u32[]{:S(2)}, u32[]{:S(2)}) %all-to-all-start.6) | async-done | bytes 2097184 | tf_op jit(solution)/shard_map/all_to_all | solution.py:144
  200.0 4.8 all-to-all-start.7
  222.8 8.3 all-to-all-done.7
  266.8 10.7 %all-to-all-start.10 = ((f32[16,1,8192]{2,1,0:T(1,128)}), f32[16,1,8192]{2,1,0:T(1,128)}, u32[]{:S(2)}, u32[]{:S(2)}) async-start(f32[16,1,8192]{2,1,0:T(1,128)} %reshape.496), calls=%async_computation.10 | async-start | bytes 1048576 | tf_op jit(solution)/shard_map/all_to_all | solution.py:60
  303.8 6.7 all-to-all-done.12
  365.1 40.5 %psum.29 = f32[]{:T(128)} all-reduce(f32[]{:T(128)} %get-tuple-element.33), channel_id=1, replica_groups=mesh['base'=16,'chan'=2] {'base','chan'}, use_global_device_ids=true, to_apply=%region_3.5 | all-reduce | flops 1 | bytes 8 | tf_op jit(solution)/shard_map/psum | solution.py:109
  427.3 4.9 all-to-all-start.14
  458.3 6.7 all-to-all-done.16
  611.2 6.7 all-to-all-done.20
  672.8 40.5 %psum.30 = f32[]{:T(128)} all-reduce(f32[]{:T(128)} %get-tuple-element.35), channel_id=1, replica_groups=mesh['base'=16,'chan'=2] {'base','chan'}, use_global_device_ids=true, to_apply=%region_5.7 | all-reduce | flops 1 | bytes 8 | tf_op jit(solution)/shard_map/psum | solution.py:109
  735.0 4.9 all-to-all-start.22
  766.0 6.7 all-to-all-done.24
  887.6 7.3 all-to-all-done.26
  903.8 9.5 all-to-all-done.28
  955.4 40.5 %psum.31 = f32[]{:T(128)} all-reduce(f32[]{:T(128)} %get-tuple-element.37), channel_id=1, replica_groups=mesh['base'=16,'chan'=2] {'base','chan'}, use_global_device_ids=true, to_apply=%region_7.9 | all-reduce | flops 1 | bytes 8 | tf_op jit(solution)/shard_map/psum | solution.py:109
  (424 shorter events, 674.3 us)
Async XLA Ops:
  3.3 58.0 %all-to-all-start = ((s32[16,2,8]{2,1,0:T(2,128)}), s32[16,2,8]{2,1,0:T(2,128)S(1)}, u32[]{:S(2)}, u32[]{:S(2)}) async-start(s32[16,2,8]{2,1,0:T(2,128)} %reshape.396), calls=%async_computation | async-start | bytes 32768 | tf_op jit(solution)/shard_map/all_to_all | solution.py:127
  81.7 20.7 %all-to-all-start.2 = ((f32[16,1,8192]{2,1,0:T(1,128)}), f32[16,1,8192]{2,1,0:T(1,128)S(1)}, u32[]{:S(2)}, u32[]{:S(2)}) async-start(f32[16,1,8192]{2,1,0:T(1,128)} %reshape.482), calls=%async_computation.2 | async-start | bytes 1048576 | tf_op jit(solution)/shard_map/all_to_all | solution.py:60
  102.4 18.4 %all-to-all-start.4 = ((f32[16,1,8192]{2,1,0:T(1,128)}), f32[16,1,8192]{2,1,0:T(1,128)S(1)}, u32[]{:S(2)}, u32[]{:S(2)}) async-start(f32[16,1,8192]{2,1,0:T(1,128)} %reshape.486), calls=%async_computation.4 | async-start | bytes 1048576 | tf_op jit(solution)/shard_map/all_to_all | solution.py:73
  151.1 45.8 %all-to-all-start.6 = ((f32[16,2,8,8,256]{4,3,2,1,0:T(8,128)}), f32[16,2,8,8,256]{4,3,2,1,0:T(8,128)}, u32[]{:S(2)}, u32[]{:S(2)}) async-start(f32[16,2,8,8,256]{4,3,2,1,0:T(8,128)} %bitcast.810), calls=%async_computation.6 | async-start | bytes 4194304 | tf_op jit(solution)/shard_map/all_to_all | solution.py:144
  200.0 31.1 %all-to-all-start.7 = ((f32[16,2,8,8,256]{4,3,2,0,1:T(8,128)}), f32[16,2,8,8,256]{4,3,2,0,1:T(8,128)}, u32[]{:S(2)}, u32[]{:S(2)}) async-start(f32[16,2,8,8,256]{4,3,2,0,1:T(8,128)} %copy.493), calls=%async_computation.7 | async-start | bytes 4194304 | tf_op jit(solution)/shard_map/all_to_all | solution.py:143
  266.8 25.0 %all-to-all-start.10 = ((f32[16,1,8192]{2,1,0:T(1,128)}), f32[16,1,8192]{2,1,0:T(1,128)}, u32[]{:S(2)}, u32[]{:S(2)}) async-start(f32[16,1,8192]{2,1,0:T(1,128)} %reshape.496), calls=%async_computation.10 | async-start | bytes 1048576 | tf_op jit(solution)/shard_map/all_to_all | solution.py:60
  291.9 18.5 %all-to-all-start.12 = ((f32[16,1,8192]{2,1,0:T(1,128)}), f32[16,1,8192]{2,1,0:T(1,128)}, u32[]{:S(2)}, u32[]{:S(2)}) async-start(f32[16,1,8192]{2,1,0:T(1,128)} %reshape.500), calls=%async_computation.12 | async-start | bytes 1048576 | tf_op jit(solution)/shard_map/all_to_all | solution.py:73
  310.4 12.9 %all-to-all-start.11 = ((f32[2,1,65536]{2,1,0:T(1,128)}), f32[2,1,65536]{2,1,0:T(1,128)}, u32[]{:S(2)}, u32[]{:S(2)}) async-start(f32[2,1,65536]{2,1,0:T(1,128)} %reshape.498), calls=%async_computation.11 | async-start | bytes 1048576 | tf_op jit(solution)/shard_map/all_to_all | solution.py:59
  323.3 21.1 %all-to-all-start.13 = ((f32[2,1,65536]{2,1,0:T(1,128)}), f32[2,1,65536]{2,1,0:T(1,128)}, u32[]{:S(2)}, u32[]{:S(2)}) async-start(f32[2,1,65536]{2,1,0:T(1,128)} %reshape.502), calls=%async_computation.13 | async-start | bytes 1048576 | tf_op jit(solution)/shard_map/all_to_all | solution.py:72
  427.3 19.2 %all-to-all-start.14 = ((f32[16,1,8192]{2,1,0:T(1,128)}), f32[16,1,8192]{2,1,0:T(1,128)}, u32[]{:S(2)}, u32[]{:S(2)}) async-start(f32[16,1,8192]{2,1,0:T(1,128)} %reshape.504), calls=%async_computation.14 | async-start | bytes 1048576 | tf_op jit(solution)/shard_map/all_to_all | solution.py:60
  446.5 18.5 %all-to-all-start.16 = ((f32[16,1,8192]{2,1,0:T(1,128)}), f32[16,1,8192]{2,1,0:T(1,128)}, u32[]{:S(2)}, u32[]{:S(2)}) async-start(f32[16,1,8192]{2,1,0:T(1,128)} %reshape.508), calls=%async_computation.16 | async-start | bytes 1048576 | tf_op jit(solution)/shard_map/all_to_all | solution.py:73
  465.0 13.0 %all-to-all-start.15 = ((f32[2,1,65536]{2,1,0:T(1,128)}), f32[2,1,65536]{2,1,0:T(1,128)}, u32[]{:S(2)}, u32[]{:S(2)}) async-start(f32[2,1,65536]{2,1,0:T(1,128)} %reshape.506), calls=%async_computation.15 | async-start | bytes 1048576 | tf_op jit(solution)/shard_map/all_to_all | solution.py:59
  478.1 21.2 %all-to-all-start.17 = ((f32[2,1,65536]{2,1,0:T(1,128)}), f32[2,1,65536]{2,1,0:T(1,128)}, u32[]{:S(2)}, u32[]{:S(2)}) async-start(f32[2,1,65536]{2,1,0:T(1,128)} %reshape.510), calls=%async_computation.17 | async-start | bytes 1048576 | tf_op jit(solution)/shard_map/all_to_all | solution.py:72
  580.5 18.8 %all-to-all-start.18 = ((f32[16,1,8192]{2,1,0:T(1,128)}), f32[16,1,8192]{2,1,0:T(1,128)}, u32[]{:S(2)}, u32[]{:S(2)}) async-start(f32[16,1,8192]{2,1,0:T(1,128)} %reshape.512), calls=%async_computation.18 | async-start | bytes 1048576 | tf_op jit(solution)/shard_map/all_to_all | solution.py:60
  599.3 18.5 %all-to-all-start.20 = ((f32[16,1,8192]{2,1,0:T(1,128)}), f32[16,1,8192]{2,1,0:T(1,128)}, u32[]{:S(2)}, u32[]{:S(2)}) async-start(f32[16,1,8192]{2,1,0:T(1,128)} %reshape.516), calls=%async_computation.20 | async-start | bytes 1048576 | tf_op jit(solution)/shard_map/all_to_all | solution.py:73
  617.9 13.1 %all-to-all-start.19 = ((f32[2,1,65536]{2,1,0:T(1,128)}), f32[2,1,65536]{2,1,0:T(1,128)}, u32[]{:S(2)}, u32[]{:S(2)}) async-start(f32[2,1,65536]{2,1,0:T(1,128)} %reshape.514), calls=%async_computation.19 | async-start | bytes 1048576 | tf_op jit(solution)/shard_map/all_to_all | solution.py:59
  631.0 21.1 %all-to-all-start.21 = ((f32[2,1,65536]{2,1,0:T(1,128)}), f32[2,1,65536]{2,1,0:T(1,128)}, u32[]{:S(2)}, u32[]{:S(2)}) async-start(f32[2,1,65536]{2,1,0:T(1,128)} %reshape.518), calls=%async_computation.21 | async-start | bytes 1048576 | tf_op jit(solution)/shard_map/all_to_all | solution.py:72
  735.0 19.2 %all-to-all-start.22 = ((f32[16,1,8192]{2,1,0:T(1,128)}), f32[16,1,8192]{2,1,0:T(1,128)}, u32[]{:S(2)}, u32[]{:S(2)}) async-start(f32[16,1,8192]{2,1,0:T(1,128)} %reshape.520), calls=%async_computation.22 | async-start | bytes 1048576 | tf_op jit(solution)/shard_map/all_to_all | solution.py:60
  754.2 18.5 %all-to-all-start.24 = ((f32[16,1,8192]{2,1,0:T(1,128)}), f32[16,1,8192]{2,1,0:T(1,128)}, u32[]{:S(2)}, u32[]{:S(2)}) async-start(f32[16,1,8192]{2,1,0:T(1,128)} %reshape.524), calls=%async_computation.24 | async-start | bytes 1048576 | tf_op jit(solution)/shard_map/all_to_all | solution.py:73
  772.7 13.0 %all-to-all-start.23 = ((f32[2,1,65536]{2,1,0:T(1,128)}), f32[2,1,65536]{2,1,0:T(1,128)}, u32[]{:S(2)}, u32[]{:S(2)}) async-start(f32[2,1,65536]{2,1,0:T(1,128)} %reshape.522), calls=%async_computation.23 | async-start | bytes 1048576 | tf_op jit(solution)/shard_map/all_to_all | solution.py:59
  785.8 21.2 %all-to-all-start.25 = ((f32[2,1,65536]{2,1,0:T(1,128)}), f32[2,1,65536]{2,1,0:T(1,128)}, u32[]{:S(2)}, u32[]{:S(2)}) async-start(f32[2,1,65536]{2,1,0:T(1,128)} %reshape.526), calls=%async_computation.25 | async-start | bytes 1048576 | tf_op jit(solution)/shard_map/all_to_all | solution.py:72
  876.3 18.6 %all-to-all-start.26 = ((f32[16,1,8192]{2,1,0:T(1,128)}), f32[16,1,8192]{2,1,0:T(1,128)S(1)}, u32[]{:S(2)}, u32[]{:S(2)}) async-start(f32[16,1,8192]{2,1,0:T(1,128)} %reshape.528), calls=%async_computation.26 | async-start | bytes 1048576 | tf_op jit(solution)/shard_map/all_to_all | solution.py:60
  894.9 18.4 %all-to-all-start.28 = ((f32[16,1,8192]{2,1,0:T(1,128)}), f32[16,1,8192]{2,1,0:T(1,128)S(1)}, u32[]{:S(2)}, u32[]{:S(2)}) async-start(f32[16,1,8192]{2,1,0:T(1,128)} %reshape.532), calls=%async_computation.28 | async-start | bytes 1048576 | tf_op jit(solution)/shard_map/all_to_all | solution.py:73
  925.6 13.4 %all-to-all-start.29 = ((f32[2,1,65536]{2,1,0:T(1,128)}), f32[2,1,65536]{2,1,0:T(1,128)}, u32[]{:S(2)}, u32[]{:S(2)}) async-start(f32[2,1,65536]{2,1,0:T(1,128)} %reshape.534), calls=%async_computation.29 | async-start | bytes 1048576 | tf_op jit(solution)/shard_map/all_to_all | solution.py:72
  (23 other events, 103.6 us)
where the time goes:
time: 1010 us; the launch traced here: 999 us
  local copies, waits for them, and re-layouts  273 us (27%)
  matrix products  192 us (19%)
  blocking collectives  172 us (17%)
  starting transfers between devices  136 us (13%)
  waiting for transfers between devices  126 us (12%)
  other arithmetic  94.2 us (9%)
    psum x4, blocking collectives, total_squares(): return lax.psum(jnp.sum(image * image), ('base', 'chan'))  162 us
    unnamed x92, local copies, waits for them, and re-layouts  85.7 us
    all_to_all x6, waiting for transfers between devices, transpose_global(): lax.all_to_all(imag_part.reshape(1, row_count, n_base, n_chan, width), 'b...  45.5 us
    all_to_all x6, starting transfers between devices, transpose_global(): lax.all_to_all(real_part.reshape(1, row_count, n_base, n_chan, width), 'b...  35.7 us
    all_to_all x6, waiting for transfers between devices, transpose_global(): lax.all_to_all(real_part.reshape(1, row_count, n_base, n_chan, width), 'b...  31.4 us
    dot_general x12, matrix products, transform_rows(): jnp.einsum('jp,rkp->rjk', sin_p, turned_im, precision=PRECISION_LEVEL)  27.9 us
    all_to_all x6, starting transfers between devices, transpose_global(): lax.all_to_all(imag_part.reshape(1, row_count, n_base, n_chan, width), 'b...  25.3 us
    dot_general x12, matrix products, transform_rows(): jnp.einsum('kq,rqp->rkp', sin_q, real_in, precision=PRECISION_LEVEL)  24.4 us
  transfers between devices with their start and end apart: 29, of which 21 were waited for; matrix products, arithmetic and copies ran while one was open for 27% of the time, Pallas kernels for 0%

commit v1 on v0

--- a/solution.py
+++ b/solution.py
@@ -70,12 +70,20 @@
             tiled=True,
         ),
         lax.all_to_all(
-            lax.all_to_all(
-                imag_part.reshape(1, row_count, n_base, n_chan, width),
-                "base",
-                split_axis=2,
-                concat_axis=0,
-                tiled=True,
+            jnp.concatenate(
+                lax.all_to_all(
+                    jnp.stack(
+                        jnp.split(
+                            imag_part.reshape(1, row_count, n_base, n_chan, width),
+                            lax.axis_size("base"),
+                            axis=2,
+                        )
+                    ),
+                    "base",
+                    0,
+                    0,
+                ),
+                axis=0,
             ),
             "chan",
             split_axis=3,

time: 1010 us -> 1100 us (1.089)
  local copies, waits for them, and re-layouts: 273 us -> 376 us
  matrix products: 192 us -> 176 us
    unnamed x92 -> x306, local copies, waits for them, and re-layouts: 85.7 us -> 195 us
    mul x9 -> x3, local copies, waits for them, and re-layouts: 20.7 us -> 7.06 us  [transform_rows(): last_im.reshape(row_count, length) * factor]
  transfers between devices with their start and end apart: 29 -> 29, of which waited for: 21 -> 18; matrix products, arithmetic and copies ran while one was open for 27% -> 31% of each run, Pallas kernels for 0% -> 0%
where the time goes in v1:
time: 1100 us; the launch traced here: 1090 us
  local copies, waits for them, and re-layouts  376 us (34%)
  matrix products  176 us (16%)
  blocking collectives  172 us (16%)
  starting transfers between devices  142 us (13%)
  waiting for transfers between devices  123 us (11%)
  other arithmetic  90 us (8%)
    unnamed x306, local copies, waits for them, and re-layouts  195 us
    psum x4, blocking collectives, total_squares(): return lax.psum(jnp.sum(image * image), ('base', 'chan'))  162 us
    all_to_all x6, waiting for transfers between devices, transpose_global(): lax.all_to_all(jnp.stack(jnp.split(imag_part.reshape(1, row_count, n_base...  49.5 us
    all_to_all x6, starting transfers between devices, transpose_global(): lax.all_to_all(real_part.reshape(1, row_count, n_base, n_chan, width), 'b...  34.1 us
    all_to_all x6, starting transfers between devices, transpose_global(): lax.all_to_all(jnp.stack(jnp.split(imag_part.reshape(1, row_count, n_base...  32.7 us
    dot_general x12, matrix products, transform_rows(): jnp.einsum('jp,rkp->rjk', sin_p, turned_im, precision=PRECISION_LEVEL)  26.7 us
    all_to_all x6, starting transfers between devices, transpose_global(): lax.all_to_all(lax.all_to_all(real_part.reshape(1, row_count, n_base, n_c...  23.8 us
    dot_general x9, matrix products, transform_rows(): jnp.einsum('kq,rqp->rkp', sin_q, imag_in, precision=PRECISION_LEVEL)  23.1 us
  transfers between devices with their start and end apart: 29, of which 18 were waited for; matrix products, arithmetic and copies ran while one was open for 31% of the time, Pallas kernels for 0%

profile of v1, /device:TPU:0, one launch (start us, length us, event | category | flops | bytes accessed | tf_op | source)
XLA Modules:
  0.0 1085.4 jit_solution(7341168562022338400)
XLA Ops:
  3.1 7.4 all-to-all-start
  13.8 40.9 %psum.28 = f32[]{:T(128)} all-reduce(f32[]{:T(128)} %multiply_reduce_fusion.3), channel_id=1, replica_groups=mesh['base'=16,'chan'=2] {'base','chan'}, use_global_device_ids=true, to_apply=%region_1.0 | all-reduce | flops 1 | bytes 8 | tf_op jit(solution)/shard_map/psum | solution.py:117
  76.8 4.9 all-to-all-start.8
  94.1 11.8 %all-to-all-done.2 = f32[16,1,8192]{2,1,0:T(1,128)S(1)} async-done(((f32[16,1,8192]{2,1,0:T(1,128)}), f32[16,1,8192]{2,1,0:T(1,128)S(1)}, u32[]{:S(2)}, u32[]{:S(2)}) %all-to-all-start.2) | async-done | bytes 524320 | tf_op jit(solution)/shard_map/all_to_all | solution.py:60
  115.0 9.4 all-to-all-done.4
  137.2 7.1 all-to-all-done.3
  144.4 10.1 all_to_all.348
  178.4 21.9 %all-to-all-done.6 = f32[16,2,8,8,256]{4,3,2,1,0:T(8,128)} async-done(((f32[16,2,8,8,256]{4,3,2,1,0:T(8,128)}), f32[16,2,8,8,256]{4,3,2,1,0:T(8,128)}, u32[]{:S(2)}, u32[]{:S(2)}) %all-to-all-start.6) | async-done | bytes 2097184 | tf_op jit(solution)/shard_map/all_to_all | solution.py:152
  226.2 8.3 all-to-all-done.7
  273.0 11.2 %all-to-all-start.10 = ((f32[16,1,8192]{2,1,0:T(1,128)}), f32[16,1,8192]{2,1,0:T(1,128)S(1)}, u32[]{:S(2)}, u32[]{:S(2)}) async-start(f32[16,1,8192]{2,1,0:T(1,128)} %reshape.520), calls=%async_computation.10 | async-start | bytes 1048576 | tf_op jit(solution)/shard_map/all_to_all | solution.py:60
  314.4 6.2 all-to-all-start.12
  327.2 7.6 all-to-all-done.12
  389.5 40.5 %psum.29 = f32[]{:T(128)} all-reduce(f32[]{:T(128)} %get-tuple-element.129), channel_id=1, replica_groups=mesh['base'=16,'chan'=2] {'base','chan'}, use_global_device_ids=true, to_apply=%region_3.5 | all-reduce | flops 1 | bytes 8 | tf_op jit(solution)/shard_map/psum | solution.py:117
  489.1 6.1 all-to-all-start.16
  501.8 7.6 all-to-all-done.16
  626.9 5.0 all-to-all-start.18
  662.0 6.2 all-to-all-start.20
  674.9 7.6 all-to-all-done.20
  737.4 40.5 %psum.30 = f32[]{:T(128)} all-reduce(f32[]{:T(128)} %get-tuple-element.131), channel_id=1, replica_groups=mesh['base'=16,'chan'=2] {'base','chan'}, use_global_device_ids=true, to_apply=%region_5.7 | all-reduce | flops 1 | bytes 8 | tf_op jit(solution)/shard_map/psum | solution.py:117
  837.0 6.1 all-to-all-start.24
  849.7 7.6 all-to-all-done.24
  971.2 10.4 all-to-all-done.26
  990.6 9.5 all-to-all-done.28
  1042.1 40.5 %psum.31 = f32[]{:T(128)} all-reduce(f32[]{:T(128)} %get-tuple-element.133), channel_id=1, replica_groups=mesh['base'=16,'chan'=2] {'base','chan'}, use_global_device_ids=true, to_apply=%region_7.9 | all-reduce | flops 1 | bytes 8 | tf_op jit(solution)/shard_map/psum | solution.py:117
  (644 shorter events, 744.8 us)
Async XLA Ops:
  3.1 65.5 %all-to-all-start = ((s32[16,2,8]{2,1,0:T(2,128)}), s32[16,2,8]{2,1,0:T(2,128)S(1)}, u32[]{:S(2)}, u32[]{:S(2)}) async-start(s32[16,2,8]{2,1,0:T(2,128)} %reshape.414), calls=%async_computation | async-start | bytes 32768 | tf_op jit(solution)/shard_map/all_to_all | solution.py:135
  88.1 17.8 %all-to-all-start.2 = ((f32[16,1,8192]{2,1,0:T(1,128)}), f32[16,1,8192]{2,1,0:T(1,128)S(1)}, u32[]{:S(2)}, u32[]{:S(2)}) async-start(f32[16,1,8192]{2,1,0:T(1,128)} %reshape.506), calls=%async_computation.2 | async-start | bytes 1048576 | tf_op jit(solution)/shard_map/all_to_all | solution.py:60
  106.0 18.4 %all-to-all-start.4 = ((f32[16,1,8192]{2,1,0:T(1,128)}), f32[16,1,8192]{2,1,0:T(1,128)S(1)}, u32[]{:S(2)}, u32[]{:S(2)}) async-start(f32[16,1,8192]{2,1,0:T(1,128)} %reshape.510), calls=%async_computation.4 | async-start | bytes 1048576 | tf_op jit(solution)/shard_map/all_to_all | solution.py:74
  154.5 45.8 %all-to-all-start.6 = ((f32[16,2,8,8,256]{4,3,2,1,0:T(8,128)}), f32[16,2,8,8,256]{4,3,2,1,0:T(8,128)}, u32[]{:S(2)}, u32[]{:S(2)}) async-start(f32[16,2,8,8,256]{4,3,2,1,0:T(8,128)} %bitcast.972), calls=%async_computation.6 | async-start | bytes 4194304 | tf_op jit(solution)/shard_map/all_to_all | solution.py:152
  203.4 31.2 %all-to-all-start.7 = ((f32[16,2,8,8,256]{4,3,2,0,1:T(8,128)}), f32[16,2,8,8,256]{4,3,2,0,1:T(8,128)}, u32[]{:S(2)}, u32[]{:S(2)}) async-start(f32[16,2,8,8,256]{4,3,2,0,1:T(8,128)} %copy.868), calls=%async_computation.7 | async-start | bytes 4194304 | tf_op jit(solution)/shard_map/all_to_all | solution.py:151
  273.0 41.3 %all-to-all-start.10 = ((f32[16,1,8192]{2,1,0:T(1,128)}), f32[16,1,8192]{2,1,0:T(1,128)S(1)}, u32[]{:S(2)}, u32[]{:S(2)}) async-start(f32[16,1,8192]{2,1,0:T(1,128)} %reshape.520), calls=%async_computation.10 | async-start | bytes 1048576 | tf_op jit(solution)/shard_map/all_to_all | solution.py:60
  314.4 20.5 %all-to-all-start.12 = ((f32[16,1,8192]{2,1,0:T(1,128)}), f32[16,1,8192]{2,1,0:T(1,128)}, u32[]{:S(2)}, u32[]{:S(2)}) async-start(f32[16,1,8192]{2,1,0:T(1,128)} %reshape.524), calls=%async_computation.12 | async-start | bytes 1048576 | tf_op jit(solution)/shard_map/all_to_all | solution.py:74
  334.9 12.9 %all-to-all-start.11 = ((f32[2,1,65536]{2,1,0:T(1,128)}), f32[2,1,65536]{2,1,0:T(1,128)}, u32[]{:S(2)}, u32[]{:S(2)}) async-start(f32[2,1,65536]{2,1,0:T(1,128)} %reshape.522), calls=%async_computation.11 | async-start | bytes 1048576 | tf_op jit(solution)/shard_map/all_to_all | solution.py:59
  347.7 21.1 %all-to-all-start.13 = ((f32[2,1,65536]{2,1,0:T(1,128)}), f32[2,1,65536]{2,1,0:T(1,128)}, u32[]{:S(2)}, u32[]{:S(2)}) async-start(f32[2,1,65536]{2,1,0:T(1,128)} %reshape.526), calls=%async_computation.13 | async-start | bytes 1048576 | tf_op jit(solution)/shard_map/all_to_all | solution.py:72
  454.1 34.9 %all-to-all-start.14 = ((f32[16,1,8192]{2,1,0:T(1,128)}), f32[16,1,8192]{2,1,0:T(1,128)S(1)}, u32[]{:S(2)}, u32[]{:S(2)}) async-start(f32[16,1,8192]{2,1,0:T(1,128)} %reshape.528), calls=%async_computation.14 | async-start | bytes 1048576 | tf_op jit(solution)/shard_map/all_to_all | solution.py:60
  489.1 20.4 %all-to-all-start.16 = ((f32[16,1,8192]{2,1,0:T(1,128)}), f32[16,1,8192]{2,1,0:T(1,128)}, u32[]{:S(2)}, u32[]{:S(2)}) async-start(f32[16,1,8192]{2,1,0:T(1,128)} %reshape.532), calls=%async_computation.16 | async-start | bytes 1048576 | tf_op jit(solution)/shard_map/all_to_all | solution.py:74
  509.5 12.9 %all-to-all-start.15 = ((f32[2,1,65536]{2,1,0:T(1,128)}), f32[2,1,65536]{2,1,0:T(1,128)}, u32[]{:S(2)}, u32[]{:S(2)}) async-start(f32[2,1,65536]{2,1,0:T(1,128)} %reshape.530), calls=%async_computation.15 | async-start | bytes 1048576 | tf_op jit(solution)/shard_map/all_to_all | solution.py:59
  522.3 21.1 %all-to-all-start.17 = ((f32[2,1,65536]{2,1,0:T(1,128)}), f32[2,1,65536]{2,1,0:T(1,128)}, u32[]{:S(2)}, u32[]{:S(2)}) async-start(f32[2,1,65536]{2,1,0:T(1,128)} %reshape.534), calls=%async_computation.17 | async-start | bytes 1048576 | tf_op jit(solution)/shard_map/all_to_all | solution.py:72
  626.9 35.1 %all-to-all-start.18 = ((f32[16,1,8192]{2,1,0:T(1,128)}), f32[16,1,8192]{2,1,0:T(1,128)S(1)}, u32[]{:S(2)}, u32[]{:S(2)}) async-start(f32[16,1,8192]{2,1,0:T(1,128)} %reshape.536), calls=%async_computation.18 | async-start | bytes 1048576 | tf_op jit(solution)/shard_map/all_to_all | solution.py:60
  662.0 20.5 %all-to-all-start.20 = ((f32[16,1,8192]{2,1,0:T(1,128)}), f32[16,1,8192]{2,1,0:T(1,128)}, u32[]{:S(2)}, u32[]{:S(2)}) async-start(f32[16,1,8192]{2,1,0:T(1,128)} %reshape.540), calls=%async_computation.20 | async-start | bytes 1048576 | tf_op jit(solution)/shard_map/all_to_all | solution.py:74
  682.5 13.1 %all-to-all-start.19 = ((f32[2,1,65536]{2,1,0:T(1,128)}), f32[2,1,65536]{2,1,0:T(1,128)}, u32[]{:S(2)}, u32[]{:S(2)}) async-start(f32[2,1,65536]{2,1,0:T(1,128)} %reshape.538), calls=%async_computation.19 | async-start | bytes 1048576 | tf_op jit(solution)/shard_map/all_to_all | solution.py:59
  695.6 21.1 %all-to-all-start.21 = ((f32[2,1,65536]{2,1,0:T(1,128)}), f32[2,1,65536]{2,1,0:T(1,128)}, u32[]{:S(2)}, u32[]{:S(2)}) async-start(f32[2,1,65536]{2,1,0:T(1,128)} %reshape.542), calls=%async_computation.21 | async-start | bytes 1048576 | tf_op jit(solution)/shard_map/all_to_all | solution.py:72
  802.1 34.9 %all-to-all-start.22 = ((f32[16,1,8192]{2,1,0:T(1,128)}), f32[16,1,8192]{2,1,0:T(1,128)S(1)}, u32[]{:S(2)}, u32[]{:S(2)}) async-start(f32[16,1,8192]{2,1,0:T(1,128)} %reshape.544), calls=%async_computation.22 | async-start | bytes 1048576 | tf_op jit(solution)/shard_map/all_to_all | solution.py:60
  837.0 20.4 %all-to-all-start.24 = ((f32[16,1,8192]{2,1,0:T(1,128)}), f32[16,1,8192]{2,1,0:T(1,128)}, u32[]{:S(2)}, u32[]{:S(2)}) async-start(f32[16,1,8192]{2,1,0:T(1,128)} %reshape.548), calls=%async_computation.24 | async-start | bytes 1048576 | tf_op jit(solution)/shard_map/all_to_all | solution.py:74
  857.4 12.9 %all-to-all-start.23 = ((f32[2,1,65536]{2,1,0:T(1,128)}), f32[2,1,65536]{2,1,0:T(1,128)}, u32[]{:S(2)}, u32[]{:S(2)}) async-start(f32[2,1,65536]{2,1,0:T(1,128)} %reshape.546), calls=%async_computation.23 | async-start | bytes 1048576 | tf_op jit(solution)/shard_map/all_to_all | solution.py:59
  870.3 21.1 %all-to-all-start.25 = ((f32[2,1,65536]{2,1,0:T(1,128)}), f32[2,1,65536]{2,1,0:T(1,128)}, u32[]{:S(2)}, u32[]{:S(2)}) async-start(f32[2,1,65536]{2,1,0:T(1,128)} %reshape.550), calls=%async_computation.25 | async-start | bytes 1048576 | tf_op jit(solution)/shard_map/all_to_all | solution.py:72
  962.6 19.1 %all-to-all-start.26 = ((f32[16,1,8192]{2,1,0:T(1,128)}), f32[16,1,8192]{2,1,0:T(1,128)S(1)}, u32[]{:S(2)}, u32[]{:S(2)}) async-start(f32[16,1,8192]{2,1,0:T(1,128)} %reshape.552), calls=%async_computation.26 | async-start | bytes 1048576 | tf_op jit(solution)/shard_map/all_to_all | solution.py:60
  981.7 18.4 %all-to-all-start.28 = ((f32[16,1,8192]{2,1,0:T(1,128)}), f32[16,1,8192]{2,1,0:T(1,128)S(1)}, u32[]{:S(2)}, u32[]{:S(2)}) async-start(f32[16,1,8192]{2,1,0:T(1,128)} %reshape.556), calls=%async_computation.28 | async-start | bytes 1048576 | tf_op jit(solution)/shard_map/all_to_all | solution.py:74
  1012.4 13.3 %all-to-all-start.29 = ((f32[2,1,65536]{2,1,0:T(1,128)}), f32[2,1,65536]{2,1,0:T(1,128)}, u32[]{:S(2)}, u32[]{:S(2)}) async-start(f32[2,1,65536]{2,1,0:T(1,128)} %reshape.558), calls=%async_computation.29 | async-start | bytes 1048576 | tf_op jit(solution)/shard_map/all_to_all | solution.py:72
  (37 other events, 607.7 us)
